TPU v7x, 32 devices: a whole 2x2x4 slice. The times are simulated.
32 devices in a mesh: groups: 2 (over y), freq: 4 (over z), space: 2 (over x), blk: 2 (over core).
Axes of the slice: x: 2, y: 2, z: 4, core: 2. Of those that a mesh axis runs over, the one named last changes fastest.
Arguments:
- realizations: bfloat16 [16, 64, 2, 8192], P('freq', 'groups', None, ('space', 'blk')), parts along dimension 1, may hold values from -6 to 6
- weights: float32 [16384], P(('groups', 'space', 'blk')), parts along dimension 0, may hold values from 0.25 to 4
- partners: int32 [3, 4], replicated, may hold values from 0 to 3, each once within a row
- block_count: int32 [2], P('groups'), parts along dimension 0, may hold values from 16 to 32
Outputs:
- modes: bfloat16 [16, 64, 2, 8192], P('freq', 'groups', None, ('space', 'blk')), parts along dimension 1
- gram: float32 [6, 16, 4, 2, 32, 32], P('groups', 'freq'), parts along dimension 0
There are 2 independent parts, one for each index of `groups`. A program takes and returns all parts, laid end to end along the dimension named above; an argument that names none is the same for every part. Nothing has to cross between parts.
Inputs may be any that keep to these rules, and one draw needn't show every extreme that they name: `partners`: each row is a permutation of the groups 0 to 3. `block_count`: blocks from this index on are left out.
All inputs are finite; a program needn't handle non-finite values.
Results may differ from a plain program's by a relative error of at most 0.0057.
Values may be sent and summed in bfloat16 or wider, within the bound.
A program may use at most 128 MiB of HBM per device.

v0:
```python
import jax
import jax.numpy as jnp
from jax import lax
from jax.sharding import PartitionSpec as P


def round_tables(partners, group_index, own_rows, which_round, per_group, total_freqs):
    offsets = jnp.arange(per_group, dtype=jnp.int32)
    partner_idx = partners[which_round, group_index] * per_group + offsets
    target_idx = (own_rows[:, None] + partner_idx[None, :]) % total_freqs
    return (partner_idx, target_idx)


def body(realizations, weights, partners, block_count):
    per_group = realizations.shape[0]
    blocks = realizations.shape[1]
    points = realizations.shape[3]
    rounds = partners.shape[0]
    shard_count = lax.axis_size("freq")
    total_freqs = per_group * shard_count
    total_space = points * lax.axis_size("space") * lax.axis_size("blk")
    gram_scale = 1.0 / jnp.sqrt(jnp.float32(total_space))
    mode_scale = 1.0 / jnp.sqrt(jnp.float32(rounds * per_group * blocks))
    keeper = (jnp.arange(blocks, dtype=jnp.int32) < block_count[0]).astype(jnp.bfloat16)
    fields = realizations * keeper[None, :, None, None]
    gathered = lax.all_gather(fields, "freq", axis=0, tiled=True)
    group_index = lax.axis_index("freq")
    own_rows = group_index * per_group + jnp.arange(per_group, dtype=jnp.int32)
    first = fields.astype(jnp.float32)[:, None]
    first_real = first[:, :, :, 0]
    first_imag = first[:, :, :, 1]
    round_grams = []
    for which_round in range(rounds):
        partner_idx, target_idx = round_tables(
            partners, group_index, own_rows, which_round, per_group, total_freqs
        )
        second = gathered[partner_idx].astype(jnp.float32)[None]
        real_part = first_real * second[:, :, :, 0] - first_imag * second[:, :, :, 1]
        imag_part = first_real * second[:, :, :, 1] + first_imag * second[:, :, :, 0]
        prod_real = (real_part * weights).astype(jnp.bfloat16)
        prod_imag = (imag_part * weights).astype(jnp.bfloat16)
        targets = gathered[target_idx]
        target_real = targets[:, :, :, 0]
        target_imag = targets[:, :, :, 1]
        real_gram = jnp.einsum(
            "ijas,ijbs->ijab", prod_real, target_real, preferred_element_type=jnp.float32
        ) + jnp.einsum(
            "ijas,ijbs->ijab", prod_imag, target_imag, preferred_element_type=jnp.float32
        )
        imag_gram = jnp.einsum(
            "ijas,ijbs->ijab", prod_real, target_imag, preferred_element_type=jnp.float32
        ) - jnp.einsum(
            "ijas,ijbs->ijab", prod_imag, target_real, preferred_element_type=jnp.float32
        )
        round_grams.append(jnp.stack([real_gram, imag_gram], axis=2))
    partial_value = jnp.stack(round_grams, axis=0)
    grams = lax.psum(partial_value, ("space", "blk")) * gram_scale
    accumulated = None
    for which_round in range(rounds):
        partner_idx, target_idx = round_tables(
            partners, group_index, own_rows, which_round, per_group, total_freqs
        )
        targets = gathered[target_idx]
        target_real = targets[:, :, :, 0]
        target_imag = targets[:, :, :, 1]
        rounded = grams[which_round].astype(jnp.bfloat16)
        real_mode = jnp.einsum(
            "ijab,ijbs->ias", rounded[:, :, 0], target_real, preferred_element_type=jnp.float32
        ) - jnp.einsum(
            "ijab,ijbs->ias", rounded[:, :, 1], target_imag, preferred_element_type=jnp.float32
        )
        imag_mode = jnp.einsum(
            "ijab,ijbs->ias", rounded[:, :, 0], target_imag, preferred_element_type=jnp.float32
        ) + jnp.einsum(
            "ijab,ijbs->ias", rounded[:, :, 1], target_real, preferred_element_type=jnp.float32
        )
        term = jnp.stack([real_mode, imag_mode], axis=2)
        accumulated = term if accumulated is None else accumulated + term
    modes = (accumulated * mode_scale).astype(jnp.bfloat16)
    return (modes, grams)


def solution(mesh):
    placed = (
        P("freq", "groups", None, ("space", "blk")),
        P(("groups", "space", "blk")),
        P(),
        P("groups"),
    )
    return jax.shard_map(
        body,
        mesh=mesh,
        in_specs=placed,
        out_specs=(
            P("freq", "groups", None, ("space", "blk")),
            P("groups", "freq", None, None, None, None),
        ),
        check_vma=False,
    )
```

profile of v0, /device:TPU:0, one launch (start us, length us, event | category | flops | bytes accessed | tf_op | source)
XLA Modules:
  0.0 216.9 jit_solution(5189849193543373611)
XLA Ops:
  7.9 2.8 %bitcast_convert_fusion.3 = (f32[4,1,32,2,2048]{4,2,3,0,1:T(8,128)S(1)}, bf16[4,32,2,2048]{3,1,2,0:T(8,128)(2,1)}) fusion(bf16[32]{0:T(256)(128)(2,1)S(1)} %compare_convert_fusion, bf16[4,32,2,2048]{3,2,1,0:T(2,128)(2,1)} %param.4), kind=kLoop, calls=%fused_computation.142 | loop fusion | flops 1048576 | bytes 4194368 | tf_op jit(solution)/shard_map/broadcast_in_dim | solution.py:29
  15.1 79.3 %all-gather.2.cloned.1.call-done = bf16[16,32,2,2048]{3,1,2,0:T(8,128)(2,1)} async-done(((bf16[4,32,2,2048]{3,1,2,0:T(8,128)(2,1)}), bf16[16,32,2,2048]{3,1,2,0:T(8,128)(2,1)}) %all-gather.2.cloned.1.call-update) | async-done | bytes 4194320 | tf_op jit(solution)/shard_map/all_gather | solution.py:26
  94.4 2.8 %gather_fusion.4 = bf16[4,32,2,2048]{3,1,2,0:T(8,128)(2,1)S(1)} fusion(bf16[16,32,2,2048]{3,1,2,0:T(8,128)(2,1)} %all-gather.2.cloned.1.call-done, s32[1024]{0:T(1024)S(1)} %pad_clamp_fusion.1), kind=kCustom, calls=%fused_computation.4 | custom fusion | bytes 2097168 | tf_op jit(solution)/shard_map/gather | solution.py:37
  98.6 5.4 %gather_fusion.5 = bf16[16,32,2,2048]{3,1,2,0:T(8,128)(2,1)} fusion(bf16[16,32,2,2048]{3,1,2,0:T(8,128)(2,1)} %all-gather.2.cloned.1.call-done, s32[1024]{0:T(1024)S(1)} %pad_clamp_fusion), kind=kCustom, calls=%fused_computation.5 | custom fusion | bytes 8388672 | tf_op jit(solution)/shard_map/gather | solution.py:42
  104.0 2.6 %copy.14 = bf16[16,32,2,2048]{3,1,0,2:T(8,128)(2,1)S(1)} copy(bf16[16,32,2,2048]{3,1,2,0:T(8,128)(2,1)} %gather_fusion.5) | data formatting | bytes 8388608 | tf_op jit(solution)/shard_map/gather | solution.py:42
  106.8 1.9 fusion.20
  109.9 2.8 %gather_fusion.2 = bf16[4,32,2,2048]{3,1,2,0:T(8,128)(2,1)S(1)} fusion(bf16[16,32,2,2048]{3,1,2,0:T(8,128)(2,1)} %all-gather.2.cloned.1.call-done, s32[1024]{0:T(1024)S(1)} %pad_clamp_fusion.3), kind=kCustom, calls=%fused_computation.2 | custom fusion | bytes 2097168 | tf_op jit(solution)/shard_map/gather | solution.py:37
  114.2 5.4 %gather_fusion.3 = bf16[16,32,2,2048]{3,1,2,0:T(8,128)(2,1)} fusion(bf16[16,32,2,2048]{3,1,2,0:T(8,128)(2,1)} %all-gather.2.cloned.1.call-done, s32[1024]{0:T(1024)S(1)} %pad_clamp_fusion.2), kind=kCustom, calls=%fused_computation.3 | custom fusion | bytes 8388672 | tf_op jit(solution)/shard_map/gather | solution.py:42
  119.6 2.6 %copy.13 = bf16[16,32,2,2048]{3,1,0,2:T(8,128)(2,1)S(1)} copy(bf16[16,32,2,2048]{3,1,2,0:T(8,128)(2,1)} %gather_fusion.3) | data formatting | bytes 8388608 | tf_op jit(solution)/shard_map/gather | solution.py:42
  122.2 2.0 fusion.16
  124.2 1.9 fusion.17
  126.1 2.8 %gather_fusion = bf16[4,32,2,2048]{3,1,2,0:T(8,128)(2,1)S(1)} fusion(bf16[16,32,2,2048]{3,1,2,0:T(8,128)(2,1)} %all-gather.2.cloned.1.call-done, s32[1024]{0:T(1024)S(1)} %pad_clamp_fusion.5), kind=kCustom, calls=%fused_computation | custom fusion | bytes 2097168 | tf_op jit(solution)/shard_map/gather | solution.py:37
  130.4 4.9 %gather_fusion.1 = bf16[16,32,2,2048]{3,1,2,0:T(8,128)(2,1)} fusion(bf16[16,32,2,2048]{3,1,2,0:T(8,128)(2,1)} %all-gather.2.cloned.1.call-done, s32[1024]{0:T(1024)S(1)} %pad_clamp_fusion.4), kind=kCustom, calls=%fused_computation.1 | custom fusion | bytes 8388672 | tf_op jit(solution)/shard_map/gather | solution.py:42
  135.3 2.6 %copy.12 = bf16[16,32,2,2048]{3,1,0,2:T(8,128)(2,1)S(1)} copy(bf16[16,32,2,2048]{3,1,2,0:T(8,128)(2,1)} %gather_fusion.1) | data formatting | bytes 8388608 | tf_op jit(solution)/shard_map/gather | solution.py:42
  142.1 1.4 fusion.90
  143.6 1.7 fusion.88
  146.4 1.3 fusion.94
  147.7 1.9 fusion.92
  150.8 1.6 fusion.96
  152.6 1.4 pad_maximum_fusion
  154.0 41.5 %all-reduce.2.cloned.1.call-done = f32[3,4,4,2,32,32]{5,4,2,1,3,0:T(8,128)} async-done(((f32[3,4,4,2,32,32]{5,4,2,1,3,0:T(8,128)}), f32[3,4,4,2,32,32]{5,4,2,1,3,0:T(8,128)}) %all-reduce.2.cloned.1.call-update) | async-done | bytes 393232 | tf_op jit(solution)/shard_map/psum | solution.py:57
  195.5 1.8 broadcast_multiply_fusion
  202.4 1.3 copy.16
  208.0 2.0 copy.15
  (95 shorter events, 24.0 us)
Async XLA Ops:
  7.2 3.6 %copy-start.18 = (s32[3,4]{1,0:T(4,128)S(1)}, s32[3,4]{1,0:T(4,128)}, u32[]{:S(2)}) copy-start(s32[3,4]{1,0:T(4,128)} %param.6) | copy-start | bytes 148
  7.2 87.2 %all-gather.2.cloned.1.call-start = ((), (), s32[]{:S(2)}) async-start(), calls=%async_computation | async-start | bytes 5242880 | tf_op jit(solution)/shard_map/all_gather | solution.py:26
  10.8 184.7 %all-reduce.2.cloned.1.call-start = ((), (), s32[]{:S(2)}) async-start(), calls=%async_computation.1 | async-start | bytes 3145728 | tf_op jit(solution)/shard_map/psum | solution.py:57
  98.6 10.1 %copy-start.9 = (f32[4,32,2048]{2,1,0:T(8,128)}, f32[4,32,2048]{2,1,0:T(8,128)S(1)}, u32[]{:S(2)}) copy-start(f32[4,32,2048]{2,1,0:T(8,128)S(1)} %get-tuple-element.14) | copy-start | bytes 3145732
  104.0 2.7 %copy-start.8 = (f32[4,32,2048]{2,1,0:T(8,128)S(1)}, f32[4,32,2048]{2,1,0:T(8,128)}, u32[]{:S(2)}) copy-start(f32[4,32,2048]{2,1,0:T(8,128)} %get-tuple-element.13) | copy-start | bytes 3145732
  104.0 2.8 %copy-start.11 = (f32[4,32,2048]{2,1,0:T(8,128)S(1)}, f32[4,32,2048]{2,1,0:T(8,128)}, u32[]{:S(2)}) copy-start(f32[4,32,2048]{2,1,0:T(8,128)} %get-tuple-element.15) | copy-start | bytes 3145732
  104.0 2.8 %copy-start.19 = (f32[2048]{0:T(1024)S(1)}, f32[2048]{0:T(1024)}, u32[]{:S(2)}) copy-start(f32[2048]{0:T(1024)} %param.5) | copy-start | bytes 24580
  106.6 2.1 copy-start
  114.2 10.0 %copy-start.13 = (f32[4,32,2048]{2,1,0:T(8,128)}, f32[4,32,2048]{2,1,0:T(8,128)S(1)}, u32[]{:S(2)}) copy-start(f32[4,32,2048]{2,1,0:T(8,128)S(1)} %get-tuple-element.10) | copy-start | bytes 3145732
  119.5 2.6 %copy-start.15 = (f32[4,32,2048]{2,1,0:T(8,128)S(1)}, f32[4,32,2048]{2,1,0:T(8,128)}, u32[]{:S(2)}) copy-start(f32[4,32,2048]{2,1,0:T(8,128)} %get-tuple-element.11) | copy-start | bytes 3145732
  122.1 2.1 copy-start.3
  135.3 2.6 %copy-start.17 = (f32[4,32,2048]{2,1,0:T(8,128)S(1)}, f32[4,32,2048]{2,1,0:T(8,128)}, u32[]{:S(2)}) copy-start(f32[4,32,2048]{2,1,0:T(8,128)} %get-tuple-element.9) | copy-start | bytes 3145732
  137.9 12.9 %copy-start.6 = (bf16[16,32,2,2048]{3,1,0,2:T(8,128)(2,1)}, bf16[16,32,2,2048]{3,1,0,2:T(8,128)(2,1)S(1)}, u32[]{:S(2)}) copy-start(bf16[16,32,2,2048]{3,1,0,2:T(8,128)(2,1)S(1)} %copy.12) | copy-start | bytes 12582916
  139.2 2.4 %copy-start.1 = (bf16[16,32,2,2048]{3,1,0,2:T(8,128)(2,1)S(1)}, bf16[16,32,2,2048]{3,1,0,2:T(8,128)(2,1)}, u32[]{:S(2)}) copy-start(bf16[16,32,2,2048]{3,1,0,2:T(8,128)(2,1)} %copy-done) | copy-start | bytes 12582916
  139.2 2.6 %copy-start.10 = (f32[4,32,2048]{2,1,0:T(8,128)S(1)}, f32[4,32,2048]{2,1,0:T(8,128)}, u32[]{:S(2)}) copy-start(f32[4,32,2048]{2,1,0:T(8,128)} %copy-done.9) | copy-start | bytes 3145732
  139.2 3.0 %copy-start.12 = (f32[4,32,2048]{2,1,0:T(8,128)S(1)}, f32[4,32,2048]{2,1,0:T(8,128)}, u32[]{:S(2)}) copy-start(f32[4,32,2048]{2,1,0:T(8,128)} %get-tuple-element.15) | copy-start | bytes 3145732
  139.2 3.0 %copy-start.20 = (f32[4,4,32,32]{3,2,1,0:T(8,128)S(1)}, f32[4,4,32,32]{3,2,1,0:T(8,128)}, u32[]{:S(2)}) copy-start(f32[4,4,32,32]{3,2,1,0:T(8,128)} %fusion.20) | copy-start | bytes 196612
  143.5 2.2 %copy-start.4 = (bf16[16,32,2,2048]{3,1,0,2:T(8,128)(2,1)S(1)}, bf16[16,32,2,2048]{3,1,0,2:T(8,128)(2,1)}, u32[]{:S(2)}) copy-start(bf16[16,32,2,2048]{3,1,0,2:T(8,128)(2,1)} %copy-done.3) | copy-start | bytes 12582916
  143.5 2.5 %copy-start.14 = (f32[4,32,2048]{2,1,0:T(8,128)S(1)}, f32[4,32,2048]{2,1,0:T(8,128)}, u32[]{:S(2)}) copy-start(f32[4,32,2048]{2,1,0:T(8,128)} %copy-done.13) | copy-start | bytes 3145732
  143.6 2.8 %copy-start.16 = (f32[4,32,2048]{2,1,0:T(8,128)S(1)}, f32[4,32,2048]{2,1,0:T(8,128)}, u32[]{:S(2)}) copy-start(f32[4,32,2048]{2,1,0:T(8,128)} %get-tuple-element.11) | copy-start | bytes 3145732
  143.6 2.8 %copy-start.22 = (f32[4,4,32,32]{3,2,1,0:T(8,128)S(1)}, f32[4,4,32,32]{3,2,1,0:T(8,128)}, u32[]{:S(2)}) copy-start(f32[4,4,32,32]{3,2,1,0:T(8,128)} %fusion.16) | copy-start | bytes 196612
  195.5 2.7 %copy-start.2 = (bf16[16,32,2,2048]{3,1,0,2:T(8,128)(2,1)S(1)}, bf16[16,32,2,2048]{3,1,0,2:T(8,128)(2,1)}, u32[]{:S(2)}) copy-start(bf16[16,32,2,2048]{3,1,0,2:T(8,128)(2,1)} %copy-done) | copy-start | bytes 12582916
  197.3 2.4 %copy-start.5 = (bf16[16,32,2,2048]{3,1,0,2:T(8,128)(2,1)S(1)}, bf16[16,32,2,2048]{3,1,0,2:T(8,128)(2,1)}, u32[]{:S(2)}) copy-start(bf16[16,32,2,2048]{3,1,0,2:T(8,128)(2,1)} %copy-done.3) | copy-start | bytes 12582916
  198.7 2.4 %copy-start.7 = (bf16[16,32,2,2048]{3,1,0,2:T(8,128)(2,1)S(1)}, bf16[16,32,2,2048]{3,1,0,2:T(8,128)(2,1)}, u32[]{:S(2)}) copy-start(bf16[16,32,2,2048]{3,1,0,2:T(8,128)(2,1)} %copy-done.6) | copy-start | bytes 12582916
  (1 other events, 1.3 us)
Sparse Core Ops, SparseCore 0:
  10.9 83.4 all-gather.1
  154.1 41.3 all-reduce.1
where the time goes:
time: 217 us
  waiting for transfers between devices  121 us (56%)
  local copies, waits for them, and re-layouts  45.3 us (21%)
  matrix products  25.9 us (12%)
  between operations  17 us (8%)
  other arithmetic  7.77 us (4%)
    all_gather x1, waiting for transfers between devices, body(): gathered = lax.all_gather(fields, 'freq', axis=0, tiled=True)  79.3 us
    psum x1, waiting for transfers between devices, body(): grams = lax.psum(partial_value, ('space', 'blk')) * gram_scale  41.5 us
    gather x6, local copies, waits for them, and re-layouts, body(): targets = gathered[target_idx]  23.5 us
    gather x3, local copies, waits for them, and re-layouts, body(): second = gathered[partner_idx].astype(jnp.float32)[None]  8.4 us
    unnamed x48, local copies, waits for them, and re-layouts  7.75 us
    dot_general x3, matrix products, body(): jnp.einsum('ijas,ijbs->ijab', prod_real, target_imag, preferred_element_t...  5.19 us
    dot_general x3, matrix products, body(): jnp.einsum('ijas,ijbs->ijab', prod_imag, target_imag, preferred_element_t...  5.13 us
    mul x4, local copies, waits for them, and re-layouts, body(): first_real * second[:, :, :, 0] - first_imag * second[:, :, :, 1]  4.69 us
  transfers between devices with their start and end apart: 2, of which 2 were waited for; matrix products, arithmetic and copies ran while one was open for 1% of the time, Pallas kernels for 0%

commit v1 on v0

--- a/solution.py
+++ b/solution.py
@@ -54,7 +54,7 @@
         )
         round_grams.append(jnp.stack([real_gram, imag_gram], axis=2))
     partial_value = jnp.stack(round_grams, axis=0)
-    grams = lax.psum(partial_value, ("space", "blk")) * gram_scale
+    grams = jnp.sum(lax.all_gather(partial_value, ("space", "blk")), axis=0) * gram_scale
     accumulated = None
     for which_round in range(rounds):
         partner_idx, target_idx = round_tables(

time: 217 us -> 225 us (1.037)
  waiting for transfers between devices: 121 us -> 124 us
  local copies, waits for them, and re-layouts: 45.3 us -> 47.8 us
    all_gather x0 -> x1, waiting for transfers between devices: none -> 45.1 us  [body(): lax.all_gather(partial_value, ('space', 'blk'))]
    psum x1 -> x0, waiting for transfers between devices: 41.5 us -> none  [body(): grams = lax.psum(partial_value, ('space', 'blk')) * gram_scale]
    reduce_sum x0 -> x1, other arithmetic: none -> 3.8 us  [body(): jnp.sum(lax.all_gather(partial_value, ('space', 'blk')), axis=0)]
where the time goes in v1:
time: 225 us; the launch traced here: 224 us
  waiting for transfers between devices  124 us (55%)
  local copies, waits for them, and re-layouts  47.8 us (21%)
  matrix products  26 us (12%)
  between operations  17.1 us (8%)
  other arithmetic  8.87 us (4%)
    all_gather x1, waiting for transfers between devices, body(): gathered = lax.all_gather(fields, 'freq', axis=0, tiled=True)  79.3 us
    all_gather x1, waiting for transfers between devices, body(): lax.all_gather(partial_value, ('space', 'blk'))  45.1 us
    gather x6, local copies, waits for them, and re-layouts, body(): targets = gathered[target_idx]  23.6 us
    unnamed x48, local copies, waits for them, and re-layouts  8.77 us
    gather x3, local copies, waits for them, and re-layouts, body(): second = gathered[partner_idx].astype(jnp.float32)[None]  8.4 us
    dot_general x3, matrix products, body(): jnp.einsum('ijas,ijbs->ijab', prod_real, target_imag, preferred_element_t...  5.3 us
    dot_general x3, matrix products, body(): jnp.einsum('ijas,ijbs->ijab', prod_imag, target_imag, preferred_element_t...  5.13 us
    mul x4, local copies, waits for them, and re-layouts, body(): first_real * second[:, :, :, 0] - first_imag * second[:, :, :, 1]  4.68 us
  transfers between devices with their start and end apart: 2, of which 2 were waited for; matrix products, arithmetic and copies ran while one was open for 1% of the time, Pallas kernels for 0%

profile of v1, /device:TPU:0, one launch (start us, length us, event | category | flops | bytes accessed | tf_op | source)
XLA Modules:
  0.0 224.1 jit_solution(9929250113062392584)
XLA Ops:
  7.9 2.8 %bitcast_convert_fusion.3 = (f32[4,1,32,2,2048]{4,2,3,0,1:T(8,128)S(1)}, bf16[4,32,2,2048]{3,1,2,0:T(8,128)(2,1)}) fusion(bf16[32]{0:T(256)(128)(2,1)S(1)} %compare_convert_fusion, bf16[4,32,2,2048]{3,2,1,0:T(2,128)(2,1)} %param.4), kind=kLoop, calls=%fused_computation.143 | loop fusion | flops 1048576 | bytes 4194368 | tf_op jit(solution)/shard_map/broadcast_in_dim | solution.py:29
  15.1 79.3 %all-gather.4.cloned.1.call-done = bf16[16,32,2,2048]{3,1,2,0:T(8,128)(2,1)} async-done(((bf16[4,32,2,2048]{3,1,2,0:T(8,128)(2,1)}), bf16[16,32,2,2048]{3,1,2,0:T(8,128)(2,1)}) %all-gather.4.cloned.1.call-update) | async-done | bytes 4194320 | tf_op jit(solution)/shard_map/all_gather | solution.py:26
  94.4 2.8 %gather_fusion.4 = bf16[4,32,2,2048]{3,1,2,0:T(8,128)(2,1)S(1)} fusion(bf16[16,32,2,2048]{3,1,2,0:T(8,128)(2,1)} %all-gather.4.cloned.1.call-done, s32[1024]{0:T(1024)S(1)} %pad_clamp_fusion.1), kind=kCustom, calls=%fused_computation.4 | custom fusion | bytes 2097168 | tf_op jit(solution)/shard_map/gather | solution.py:37
  98.6 5.4 %gather_fusion.5 = bf16[16,32,2,2048]{3,1,2,0:T(8,128)(2,1)} fusion(bf16[16,32,2,2048]{3,1,2,0:T(8,128)(2,1)} %all-gather.4.cloned.1.call-done, s32[1024]{0:T(1024)S(1)} %pad_clamp_fusion), kind=kCustom, calls=%fused_computation.5 | custom fusion | bytes 8388672 | tf_op jit(solution)/shard_map/gather | solution.py:42
  104.0 2.6 %copy.21 = bf16[16,32,2,2048]{3,1,0,2:T(8,128)(2,1)S(1)} copy(bf16[16,32,2,2048]{3,1,2,0:T(8,128)(2,1)} %gather_fusion.5) | data formatting | bytes 8388608 | tf_op jit(solution)/shard_map/gather | solution.py:42
  106.8 2.0 fusion.20
  110.0 2.8 %gather_fusion.2 = bf16[4,32,2,2048]{3,1,2,0:T(8,128)(2,1)S(1)} fusion(bf16[16,32,2,2048]{3,1,2,0:T(8,128)(2,1)} %all-gather.4.cloned.1.call-done, s32[1024]{0:T(1024)S(1)} %pad_clamp_fusion.3), kind=kCustom, calls=%fused_computation.2 | custom fusion | bytes 2097168 | tf_op jit(solution)/shard_map/gather | solution.py:37
  114.3 5.4 %gather_fusion.3 = bf16[16,32,2,2048]{3,1,2,0:T(8,128)(2,1)} fusion(bf16[16,32,2,2048]{3,1,2,0:T(8,128)(2,1)} %all-gather.4.cloned.1.call-done, s32[1024]{0:T(1024)S(1)} %pad_clamp_fusion.2), kind=kCustom, calls=%fused_computation.3 | custom fusion | bytes 8388672 | tf_op jit(solution)/shard_map/gather | solution.py:42
  119.7 2.6 %copy.20 = bf16[16,32,2,2048]{3,1,0,2:T(8,128)(2,1)S(1)} copy(bf16[16,32,2,2048]{3,1,2,0:T(8,128)(2,1)} %gather_fusion.3) | data formatting | bytes 8388608 | tf_op jit(solution)/shard_map/gather | solution.py:42
  122.3 2.1 fusion.16
  124.4 1.9 fusion.17
  126.3 2.8 %gather_fusion = bf16[4,32,2,2048]{3,1,2,0:T(8,128)(2,1)S(1)} fusion(bf16[16,32,2,2048]{3,1,2,0:T(8,128)(2,1)} %all-gather.4.cloned.1.call-done, s32[1024]{0:T(1024)S(1)} %pad_clamp_fusion.5), kind=kCustom, calls=%fused_computation | custom fusion | bytes 2097168 | tf_op jit(solution)/shard_map/gather | solution.py:37
  130.5 5.0 %gather_fusion.1 = bf16[16,32,2,2048]{3,1,2,0:T(8,128)(2,1)} fusion(bf16[16,32,2,2048]{3,1,2,0:T(8,128)(2,1)} %all-gather.4.cloned.1.call-done, s32[1024]{0:T(1024)S(1)} %pad_clamp_fusion.4), kind=kCustom, calls=%fused_computation.1 | custom fusion | bytes 8388672 | tf_op jit(solution)/shard_map/gather | solution.py:42
  135.5 2.6 %copy.19 = bf16[16,32,2,2048]{3,1,0,2:T(8,128)(2,1)S(1)} copy(bf16[16,32,2,2048]{3,1,2,0:T(8,128)(2,1)} %gather_fusion.1) | data formatting | bytes 8388608 | tf_op jit(solution)/shard_map/gather | solution.py:42
  142.4 1.4 fusion.90
  143.8 1.7 fusion.88
  146.6 1.3 fusion.94
  147.9 1.9 fusion.92
  151.0 1.6 fusion.96
  153.0 1.3 copy.22
  154.3 45.1 %all-gather.6.cloned.1.call-done = f32[12,4,4,2,32,32]{5,4,3,2,1,0:T(8,128)} async-done(((f32[3,4,4,2,32,32]{5,4,3,2,1,0:T(8,128)}), f32[12,4,4,2,32,32]{5,4,3,2,1,0:T(8,128)}) %all-gather.6.cloned.1.call-update) | async-done | bytes 1572880 | tf_op jit(solution)/shard_map/all_gather | solution.py:57
  199.4 3.8 %reduce_sum.9 = f32[3,4,4,2,32,32]{5,4,3,2,1,0:T(8,128)S(1)} reduce(f32[4,3,4,4,2,32,32]{6,5,4,3,2,1,0:T(8,128)} %bitcast.253, f32[]{:T(128)} %constant.57.clone.1), dimensions={0}, to_apply=%region_0.1 | reduce | flops 294912 | bytes 1966084 | tf_op jit(solution)/shard_map/reduce_sum | solution.py:57
  203.6 1.8 copy-done.2
  215.2 2.0 copy.24
  (97 shorter events, 25.0 us)
Async XLA Ops:
  7.2 3.6 %copy-start.18 = (s32[3,4]{1,0:T(4,128)S(1)}, s32[3,4]{1,0:T(4,128)}, u32[]{:S(2)}) copy-start(s32[3,4]{1,0:T(4,128)} %param.6) | copy-start | bytes 148
  7.2 87.2 %all-gather.4.cloned.1.call-start = ((), (), s32[]{:S(2)}) async-start(), calls=%async_computation | async-start | bytes 5242880 | tf_op jit(solution)/shard_map/all_gather | solution.py:26
  10.8 188.7 %all-gather.6.cloned.1.call-start = ((), (), s32[]{:S(2)}) async-start(), calls=%async_computation.1 | async-start | bytes 7864320 | tf_op jit(solution)/shard_map/all_gather | solution.py:57
  98.6 10.2 %copy-start.9 = (f32[4,32,2048]{2,1,0:T(8,128)}, f32[4,32,2048]{2,1,0:T(8,128)S(1)}, u32[]{:S(2)}) copy-start(f32[4,32,2048]{2,1,0:T(8,128)S(1)} %get-tuple-element.16) | copy-start | bytes 3145732
  104.0 2.7 %copy-start.8 = (f32[4,32,2048]{2,1,0:T(8,128)S(1)}, f32[4,32,2048]{2,1,0:T(8,128)}, u32[]{:S(2)}) copy-start(f32[4,32,2048]{2,1,0:T(8,128)} %get-tuple-element.15) | copy-start | bytes 3145732
  104.0 2.8 %copy-start.11 = (f32[4,32,2048]{2,1,0:T(8,128)S(1)}, f32[4,32,2048]{2,1,0:T(8,128)}, u32[]{:S(2)}) copy-start(f32[4,32,2048]{2,1,0:T(8,128)} %get-tuple-element.17) | copy-start | bytes 3145732
  104.0 2.8 %copy-start.19 = (f32[2048]{0:T(1024)S(1)}, f32[2048]{0:T(1024)}, u32[]{:S(2)}) copy-start(f32[2048]{0:T(1024)} %param.5) | copy-start | bytes 24580
  106.6 2.2 copy-start
  114.3 10.1 %copy-start.13 = (f32[4,32,2048]{2,1,0:T(8,128)}, f32[4,32,2048]{2,1,0:T(8,128)S(1)}, u32[]{:S(2)}) copy-start(f32[4,32,2048]{2,1,0:T(8,128)S(1)} %get-tuple-element.12) | copy-start | bytes 3145732
  119.7 2.6 %copy-start.15 = (f32[4,32,2048]{2,1,0:T(8,128)S(1)}, f32[4,32,2048]{2,1,0:T(8,128)}, u32[]{:S(2)}) copy-start(f32[4,32,2048]{2,1,0:T(8,128)} %get-tuple-element.13) | copy-start | bytes 3145732
  122.3 2.1 copy-start.3
  135.5 2.6 %copy-start.17 = (f32[4,32,2048]{2,1,0:T(8,128)S(1)}, f32[4,32,2048]{2,1,0:T(8,128)}, u32[]{:S(2)}) copy-start(f32[4,32,2048]{2,1,0:T(8,128)} %get-tuple-element.11) | copy-start | bytes 3145732
  138.1 12.9 %copy-start.6 = (bf16[16,32,2,2048]{3,1,0,2:T(8,128)(2,1)}, bf16[16,32,2,2048]{3,1,0,2:T(8,128)(2,1)S(1)}, u32[]{:S(2)}) copy-start(bf16[16,32,2,2048]{3,1,0,2:T(8,128)(2,1)S(1)} %copy.19) | copy-start | bytes 12582916
  139.4 2.4 %copy-start.1 = (bf16[16,32,2,2048]{3,1,0,2:T(8,128)(2,1)S(1)}, bf16[16,32,2,2048]{3,1,0,2:T(8,128)(2,1)}, u32[]{:S(2)}) copy-start(bf16[16,32,2,2048]{3,1,0,2:T(8,128)(2,1)} %copy-done) | copy-start | bytes 12582916
  139.4 2.7 %copy-start.10 = (f32[4,32,2048]{2,1,0:T(8,128)S(1)}, f32[4,32,2048]{2,1,0:T(8,128)}, u32[]{:S(2)}) copy-start(f32[4,32,2048]{2,1,0:T(8,128)} %copy-done.9) | copy-start | bytes 3145732
  139.4 3.0 %copy-start.12 = (f32[4,32,2048]{2,1,0:T(8,128)S(1)}, f32[4,32,2048]{2,1,0:T(8,128)}, u32[]{:S(2)}) copy-start(f32[4,32,2048]{2,1,0:T(8,128)} %get-tuple-element.17) | copy-start | bytes 3145732
  139.4 3.0 %copy-start.20 = (f32[4,4,32,32]{3,2,1,0:T(8,128)S(1)}, f32[4,4,32,32]{3,2,1,0:T(8,128)}, u32[]{:S(2)}) copy-start(f32[4,4,32,32]{3,2,1,0:T(8,128)} %fusion.20) | copy-start | bytes 196612
  143.7 2.2 copy-start.4
  143.8 2.5 %copy-start.14 = (f32[4,32,2048]{2,1,0:T(8,128)S(1)}, f32[4,32,2048]{2,1,0:T(8,128)}, u32[]{:S(2)}) copy-start(f32[4,32,2048]{2,1,0:T(8,128)} %copy-done.13) | copy-start | bytes 3145732
  143.8 2.8 %copy-start.16 = (f32[4,32,2048]{2,1,0:T(8,128)S(1)}, f32[4,32,2048]{2,1,0:T(8,128)}, u32[]{:S(2)}) copy-start(f32[4,32,2048]{2,1,0:T(8,128)} %get-tuple-element.13) | copy-start | bytes 3145732
  143.8 2.8 %copy-start.22 = (f32[4,4,32,32]{3,2,1,0:T(8,128)S(1)}, f32[4,4,32,32]{3,2,1,0:T(8,128)}, u32[]{:S(2)}) copy-start(f32[4,4,32,32]{3,2,1,0:T(8,128)} %fusion.16) | copy-start | bytes 196612
  203.2 2.2 copy-start.2
  203.5 3.2 %copy-start.5 = (bf16[16,32,2,2048]{3,1,0,2:T(8,128)(2,1)S(1)}, bf16[16,32,2,2048]{3,1,0,2:T(8,128)(2,1)}, u32[]{:S(2)}) copy-start(bf16[16,32,2,2048]{3,1,0,2:T(8,128)(2,1)} %copy-done.3) | copy-start | bytes 12582916
  206.0 2.4 %copy-start.7 = (bf16[16,32,2,2048]{3,1,0,2:T(8,128)(2,1)S(1)}, bf16[16,32,2,2048]{3,1,0,2:T(8,128)(2,1)}, u32[]{:S(2)}) copy-start(bf16[16,32,2,2048]{3,1,0,2:T(8,128)(2,1)} %copy-done.6) | copy-start | bytes 12582916
  (1 other events, 1.3 us)
Sparse Core Ops, SparseCore 0:
  10.9 83.4 all-gather.3
  154.5 44.8 all-gather.5
